TPU v7x, 32 devices: a whole 2x2x4 slice. The times are simulated.
32 devices in a mesh: row: 4 (over y, x), col: 8 (over z, core).
Axes of the slice: x: 2, y: 2, z: 4, core: 2. Of those that a mesh axis runs over, the one named last changes fastest.
Arguments:
- fact_block: int32 [98304, 1], P(('row', 'col')), may hold values from 0 to 31; in each aligned block of 3072 rows (0 to 3071, 3072 to 6143, ...) at most 192 rows name the same one
- fact_offset: int32 [98304], P(('row', 'col')), may hold values from 0 to 2047
- fact_date: int32 [98304], P(('row', 'col')), may hold values from 0 to 2555
- revenue: bfloat16 [98304], P(('row', 'col')), may hold values from 0.5 to 4
- supplier_words: int32 [2208], P('col'), may hold values from 0 to 1073741823
- date_words: int32 [88], P('col'), may hold values from 0 to 1073741823
- candidates: int32 [1024], replicated, may hold values from 0 to 65535
Outputs:
- supplier_revenue: float32 [65536], P(('row', 'col'))
- candidate_revenue: float32 [1024], replicated
- candidate_total: float32 [], replicated
Inputs may be any that keep to these rules, and one draw needn't show every extreme that they name: `fact_block`: each device's rows name no owner block more than 192 times. `candidates`: ids may repeat.
All inputs are finite; a program needn't handle non-finite values.
Results may differ from a plain program's by a relative error of at most 0.0003.
Values sent between devices are 32-bit elements; how exact they have to be, the bound alone decides.
A program may use at most 64 MiB of HBM per device.

v0:
```python
import jax
import jax.numpy as jnp
from jax import lax
from jax.sharding import PartitionSpec as P

SUP_DEV = 2048


def filtered_revenue(owner, fact_offset, fact_date, revenue, supplier_all, date_all):
    words_per_block = (SUP_DEV + 29) // 30
    word_index = owner * words_per_block + fact_offset // 30
    supplier_word = jnp.take(supplier_all, word_index)
    supplier_bit = jnp.bitwise_and(jnp.right_shift(supplier_word, fact_offset % 30), 1)
    date_slot = fact_date // 30
    positions = jnp.arange(date_all.shape[0], dtype=jnp.int32)
    date_word = jnp.sum(
        jnp.where(date_slot[:, None] == positions[None, :], date_all[None, :], 0), axis=1
    )
    date_bit = jnp.bitwise_and(jnp.right_shift(date_word, fact_date % 30), 1)
    return jnp.where(supplier_bit * date_bit == 1, revenue, jnp.zeros_like(revenue))


def per_device(fact_block, fact_offset, fact_date, revenue, supplier_words, date_words, candidates):
    devices = lax.axis_size("row") * lax.axis_size("col")
    supplier_all, date_all = (
        lax.all_gather(supplier_words, "col", axis=0, tiled=True),
        lax.all_gather(date_words, "col", axis=0, tiled=True),
    )
    owner = fact_block[:, 0]
    masked = filtered_revenue(owner, fact_offset, fact_date, revenue, supplier_all, date_all)
    row_count = fact_offset.shape[0]
    capacity = max(2, 2 * row_count // devices)
    row_ids = jnp.arange(row_count, dtype=jnp.int32)
    earlier = (owner[:, None] == owner[None, :]) & (row_ids[None, :] < row_ids[:, None])
    ranking = jnp.sum(earlier, axis=1, dtype=jnp.int32)
    slot_index = owner * capacity + ranking
    slot_revenue = (
        jnp.zeros((devices * capacity,), jnp.float32).at[slot_index].set(masked.astype(jnp.float32))
    )
    slot_offset = (
        jnp.zeros((devices * capacity,), jnp.float32)
        .at[slot_index]
        .set(fact_offset.astype(jnp.float32))
    )
    payload = jnp.stack((slot_revenue, slot_offset), axis=-1)
    payload = payload.reshape(lax.axis_size("row"), lax.axis_size("col"), 2 * capacity)
    arrived = lax.all_to_all(
        lax.all_to_all(payload, "row", split_axis=0, concat_axis=0, tiled=True),
        "col",
        split_axis=1,
        concat_axis=1,
        tiled=True,
    )
    arrived = arrived.reshape(-1, 2)
    owned = jax.ops.segment_sum(
        arrived[:, 0], arrived[:, 1].astype(jnp.int32), num_segments=SUP_DEV
    )
    global_id = owner * SUP_DEV + fact_offset
    onehot_cands = (global_id[:, None] == candidates[None, :]).astype(jnp.bfloat16)
    own_terms = jnp.dot(masked[None, :], onehot_cands, preferred_element_type=jnp.float32)[0]
    candidate_revenue = lax.psum(own_terms, ("row", "col"))
    candidate_total = jnp.sum(candidate_revenue)
    return (owned, candidate_revenue, candidate_total)


def solution(mesh):
    in_specs = (
        P(("row", "col"), None),
        P(("row", "col")),
        P(("row", "col")),
        P(("row", "col")),
        P("col"),
        P("col"),
        P(),
    )
    out_specs = (P(("row", "col")), P(), P())
    return jax.shard_map(
        per_device, mesh=mesh, in_specs=in_specs, out_specs=out_specs, check_vma=False
    )
```

profile of v0, /device:TPU:20, one launch (start us, length us, event | category | flops | bytes accessed | tf_op | source)
XLA Modules:
  0.0 186.4 jit_solution(15897103582751986480)
XLA Ops:
  0.6 1.2 dynamic-slice
  3.2 3.9 %convert_reduce_fusion = s32[3072]{0:T(1024)S(1)} fusion(s32[3072]{0:T(1024)} %bitcast.11), kind=kLoop, calls=%fused_computation.4 | loop fusion | flops 47182848 | bytes 24576 | tf_op jit(solution)/shard_map/reduce_sum | solution.py:35
  7.0 0.7 compare_select_fusion
  7.8 0.7 add_select_fusion.1
  8.5 0.8 multiply_add_fusion
  9.3 0.9 dynamic-update-slice.1
  10.2 0.9 dynamic-update-slice
  11.0 21.6 %all-reduce.2 = (s32[88]{0:T(128)S(1)}, s32[2208]{0:T(1024)S(1)}) all-reduce(s32[88]{0:T(128)S(1)} %dynamic-update-slice.1, s32[2208]{0:T(1024)S(1)} %dynamic-update-slice), channel_id=1, replica_groups=mesh['row'=4,'col'=8] {'col'}, use_global_device_ids=true, to_apply=%add.1 | all-reduce | flops 2296 | bytes 18368
  32.9 17.4 %gather_fusion = s32[3072]{0:T(1024)S(1)} fusion(s32[2208]{0:T(1024)S(1)} %get-tuple-element.4, s32[3072]{0:T(1024)S(1)} %get-tuple-element.8), kind=kCustom, calls=%fused_computation | custom fusion | bytes 36864 | tf_op jit(solution)/shard_map/jit(_take)/gather | solution.py:12
  50.4 11.8 %scatter_custom_fusion = f32[6144]{0:T(1024)S(1)} fusion(s32[3072]{0:T(1024)S(1)} %bitcast.16, f32[3072]{0:T(1024)S(1)} %get-tuple-element.5, f32[]{:T(128)} %constant.30.clone.1), kind=kCustom, calls=%fused_computation.35 | custom fusion | bytes 24580 | tf_op jit(solution)/shard_map/scatter | solution.py:38
  62.2 11.8 %scatter_custom_fusion.1 = f32[6144]{0:T(1024)S(1)} fusion(s32[3072]{0:T(1024)S(1)} %bitcast.17, f32[3072]{0:T(1024)S(1)} %get-tuple-element.9, f32[]{:T(128)} %constant.30.clone.1), kind=kCustom, calls=%fused_computation.33 | custom fusion | bytes 24580 | tf_op jit(solution)/shard_map/scatter | solution.py:43
  74.1 1.1 copy.14
  75.2 2.7 %reshape.27 = f32[4,8,384]{2,1,0:T(8,128)} reshape(f32[6144,2]{1,0:T(8,128)S(1)} %copy.14) | data formatting | bytes 98304 | tf_op jit(solution)/shard_map/reshape | solution.py:46
  77.9 4.2 %all-to-all-start = ((f32[4,8,384]{2,1,0:T(8,128)}), f32[4,8,384]{2,1,0:T(8,128)S(1)}, u32[]{:S(2)}, u32[]{:S(2)}) async-start(f32[4,8,384]{2,1,0:T(8,128)} %reshape.27), calls=%async_computation | async-start | bytes 98304 | tf_op jit(solution)/shard_map/all_to_all | solution.py:48
  82.2 3.5 %all-to-all-done = f32[4,8,384]{2,1,0:T(8,128)S(1)} async-done(((f32[4,8,384]{2,1,0:T(8,128)}), f32[4,8,384]{2,1,0:T(8,128)S(1)}, u32[]{:S(2)}, u32[]{:S(2)}) %all-to-all-start) | async-done | bytes 49184 | tf_op jit(solution)/shard_map/all_to_all | solution.py:48
  85.7 0.6 copy.15
  86.3 10.8 %all-to-all-start.1 = ((f32[4,8,384]{2,0,1:T(4,128)}), f32[4,8,384]{2,0,1:T(4,128)S(1)}, u32[]{:S(2)}, u32[]{:S(2)}) async-start(f32[4,8,384]{2,0,1:T(4,128)} %copy.15), calls=%async_computation.1 | async-start | bytes 98304 | tf_op jit(solution)/shard_map/all_to_all | solution.py:47
  97.1 2.0 %fusion.1 = f32[1,1024]{1,0:T(1,128)S(1)} fusion(bf16[3072,1]{0,1:T(2,128)(2,1)S(1)} %reshape.72, s32[1024]{0:T(1024)S(1)} %copy-done.5, s32[3072]{0:T(1024)S(1)} %get-tuple-element.7), kind=kOutput, calls=%fused_computation.7 | convolution fusion | flops 9437184 | bytes 26624 | tf_op jit(solution)/shard_map/dot_general | solution.py:60
  99.1 40.9 %psum.7 = f32[1024]{0:T(1024)S(1)} all-reduce(f32[1024]{0:T(1024)S(1)} %bitcast.19), channel_id=1, replica_groups=mesh['row'=4,'col'=8] {'row','col'}, use_global_device_ids=true, to_apply=%region_5.6 | all-reduce | flops 1024 | bytes 8192 | tf_op jit(solution)/shard_map/psum | solution.py:61
  140.0 0.6 reduce_sum.32
  140.6 3.2 %reshape.28 = f32[6144,2]{1,0:T(8,128)S(1)} reshape(f32[4,8,384]{2,1,0:T(8,128)S(1)} %copy.16) | data formatting | bytes 98304 | tf_op jit(solution)/shard_map/reshape | solution.py:54
  143.7 0.9 slice_reduce_fusion
  144.6 1.7 fusion.5
  146.3 40.0 %scatter_custom_fusion.2 = f32[2048]{0:T(1024)} fusion(s32[6144]{0:T(1024)S(1)} %fusion.5, f32[6144]{0:T(1024)S(1)} %slice_reduce_fusion, f32[]{:T(128)} %constant.30.clone.1), kind=kCustom, calls=%fused_computation.43 | custom fusion | flops 6144 | bytes 8196 | tf_op jit(solution)/shard_map/scatter-add | solution.py:55
  (20 shorter events, 0.4 us)
Async XLA Ops:
  32.9 17.5 %copy-start = (s32[3072,1]{0,1:T(1,128)S(1)}, s32[3072,1]{0,1:T(1,128)}, u32[]{:S(2)}) copy-start(s32[3072,1]{0,1:T(1,128)} %param.7) | copy-start | bytes 36868
  32.9 17.5 %copy-start.1 = (s32[3072]{0:T(1024)S(1)}, s32[3072]{0:T(1024)}, u32[]{:S(2)}) copy-start(s32[3072]{0:T(1024)} %param.9) | copy-start | bytes 36868
  32.9 17.5 %copy-start.2 = (s32[3072]{0:T(1024)S(1)}, s32[3072]{0:T(1024)}, u32[]{:S(2)}) copy-start(s32[3072]{0:T(1024)} %param.8) | copy-start | bytes 36868
  32.9 17.5 %copy-start.4 = (bf16[3072]{0:T(1024)(128)(2,1)S(1)}, bf16[3072]{0:T(1024)(128)(2,1)}, u32[]{:S(2)}) copy-start(bf16[3072]{0:T(1024)(128)(2,1)} %param.10) | copy-start | bytes 18436
  74.1 23.0 %copy-start.5 = (s32[1024]{0:T(1024)S(1)}, s32[1024]{0:T(1024)}, u32[]{:S(2)}) copy-start(s32[1024]{0:T(1024)} %param.13) | copy-start | bytes 12292
  77.9 7.7 %all-to-all-start = ((f32[4,8,384]{2,1,0:T(8,128)}), f32[4,8,384]{2,1,0:T(8,128)S(1)}, u32[]{:S(2)}, u32[]{:S(2)}) async-start(f32[4,8,384]{2,1,0:T(8,128)} %reshape.27), calls=%async_computation | async-start | bytes 98304 | tf_op jit(solution)/shard_map/all_to_all | solution.py:48
  86.3 54.3 %all-to-all-start.1 = ((f32[4,8,384]{2,0,1:T(4,128)}), f32[4,8,384]{2,0,1:T(4,128)S(1)}, u32[]{:S(2)}, u32[]{:S(2)}) async-start(f32[4,8,384]{2,0,1:T(4,128)} %copy.15), calls=%async_computation.1 | async-start | bytes 98304 | tf_op jit(solution)/shard_map/all_to_all | solution.py:47
  140.0 4.7 %copy-start.3 = (f32[1024]{0:T(1024)}, f32[1024]{0:T(1024)S(1)}, u32[]{:S(2)}) copy-start(f32[1024]{0:T(1024)S(1)} %psum.7) | copy-start | bytes 12292
where the time goes:
time: 187 us; the launch traced here: 186 us
  blocking collectives  62.5 us (33%)
  local copies, waits for them, and re-layouts  52.5 us (28%)
  other arithmetic  48.8 us (26%)
  starting transfers between devices  15 us (8%)
  waiting for transfers between devices  3.5 us (2%)
  between operations  2.1 us (1%)
  matrix products  2 us (1%)
    psum x1, blocking collectives, per_device(): candidate_revenue = lax.psum(own_terms, ('row', 'col'))  40.9 us
    scatter-add x1, other arithmetic, per_device(): jax.ops.segment_sum(arrived[:, 0], arrived[:, 1].astype(jnp.int32), num_s...  40 us
    unnamed x1, blocking collectives  21.6 us
    gather x1, local copies, waits for them, and re-layouts, filtered_revenue(): supplier_word = jnp.take(supplier_all, word_index)  17.4 us
    scatter x1, local copies, waits for them, and re-layouts, per_device(): slot_offset = jnp.zeros((devices * capacity,), jnp.float32).at[slot_index...  11.8 us
    scatter x1, local copies, waits for them, and re-layouts, per_device(): jnp.zeros((devices * capacity,), jnp.float32).at[slot_index]  11.8 us
    all_to_all x1, starting transfers between devices, per_device(): lax.all_to_all(lax.all_to_all(payload, 'row', split_axis=0, concat_axis=0...  10.8 us
    all_to_all x1, starting transfers between devices, per_device(): lax.all_to_all(payload, 'row', split_axis=0, concat_axis=0, tiled=True)  4.22 us
  transfers between devices with their start and end apart: 2, of which 1 were waited for; matrix products, arithmetic and copies ran while one was open for 1% of the time, Pallas kernels for 0%

commit v1 on v0

--- a/solution.py
+++ b/solution.py
@@ -58,7 +58,7 @@
     global_id = owner * SUP_DEV + fact_offset
     onehot_cands = (global_id[:, None] == candidates[None, :]).astype(jnp.bfloat16)
     own_terms = jnp.dot(masked[None, :], onehot_cands, preferred_element_type=jnp.float32)[0]
-    candidate_revenue = lax.psum(own_terms, ("row", "col"))
+    candidate_revenue = lax.psum(lax.psum(own_terms, "row"), "col")
     candidate_total = jnp.sum(candidate_revenue)
     return (owned, candidate_revenue, candidate_total)
 

time: 187 us -> 170 us (0.909)
  the two profiles are of different devices: /device:TPU:20 before, /device:TPU:4 now
where the time goes in v1:
time: 170 us; the launch traced here: 169 us
  blocking collectives  52.9 us (31%)
  local copies, waits for them, and re-layouts  52.5 us (31%)
  other arithmetic  48.2 us (28%)
  starting transfers between devices  7.56 us (4%)
  waiting for transfers between devices  3.46 us (2%)
  between operations  2.13 us (1%)
  matrix products  2.01 us (1%)
    scatter-add x1, other arithmetic, per_device(): jax.ops.segment_sum(arrived[:, 0], arrived[:, 1].astype(jnp.int32), num_s...  39.4 us
    unnamed x1, blocking collectives  28.8 us
    psum x2, blocking collectives, per_device(): candidate_revenue = lax.psum(lax.psum(own_terms, 'row'), 'col')  24.1 us
    gather x1, local copies, waits for them, and re-layouts, filtered_revenue(): supplier_word = jnp.take(supplier_all, word_index)  17.4 us
    scatter x1, local copies, waits for them, and re-layouts, per_device(): jnp.zeros((devices * capacity,), jnp.float32).at[slot_index]  11.8 us
    scatter x1, local copies, waits for them, and re-layouts, per_device(): slot_offset = jnp.zeros((devices * capacity,), jnp.float32).at[slot_index...  11.8 us
    all_to_all x1, starting transfers between devices, per_device(): lax.all_to_all(payload, 'row', split_axis=0, concat_axis=0, tiled=True)  4.22 us
    reduce_sum x1, other arithmetic, per_device(): ranking = jnp.sum(earlier, axis=1, dtype=jnp.int32)  3.86 us
  transfers between devices with their start and end apart: 2, of which 1 were waited for; matrix products, arithmetic and copies ran while one was open for 2% of the time, Pallas kernels for 0%

profile of v1, /device:TPU:4, one launch (start us, length us, event | category | flops | bytes accessed | tf_op | source)
XLA Modules:
  0.0 168.8 jit_solution(12069964129701491362)
XLA Ops:
  0.6 1.2 dynamic-slice
  3.2 3.9 %convert_reduce_fusion = s32[3072]{0:T(1024)S(1)} fusion(s32[3072]{0:T(1024)} %bitcast.11), kind=kLoop, calls=%fused_computation.4 | loop fusion | flops 47182848 | bytes 24576 | tf_op jit(solution)/shard_map/reduce_sum | solution.py:35
  7.0 0.7 compare_select_fusion
  7.8 0.7 add_select_fusion.1
  8.5 0.8 multiply_add_fusion
  9.3 0.9 dynamic-update-slice.1
  10.2 0.9 dynamic-update-slice
  11.0 28.8 %all-reduce.2 = (s32[88]{0:T(128)S(1)}, s32[2208]{0:T(1024)S(1)}) all-reduce(s32[88]{0:T(128)S(1)} %dynamic-update-slice.1, s32[2208]{0:T(1024)S(1)} %dynamic-update-slice), channel_id=1, replica_groups=mesh['row'=4,'col'=8] {'col'}, use_global_device_ids=true, to_apply=%add.1 | all-reduce | flops 2296 | bytes 18368
  40.1 17.4 %gather_fusion = s32[3072]{0:T(1024)S(1)} fusion(s32[2208]{0:T(1024)S(1)} %get-tuple-element.4, s32[3072]{0:T(1024)S(1)} %get-tuple-element.8), kind=kCustom, calls=%fused_computation | custom fusion | bytes 36864 | tf_op jit(solution)/shard_map/jit(_take)/gather | solution.py:12
  57.6 11.8 %scatter_custom_fusion = f32[6144]{0:T(1024)S(1)} fusion(s32[3072]{0:T(1024)S(1)} %bitcast.16, f32[3072]{0:T(1024)S(1)} %get-tuple-element.5, f32[]{:T(128)} %constant.30.clone.1), kind=kCustom, calls=%fused_computation.35 | custom fusion | bytes 24580 | tf_op jit(solution)/shard_map/scatter | solution.py:38
  69.5 11.8 %scatter_custom_fusion.1 = f32[6144]{0:T(1024)S(1)} fusion(s32[3072]{0:T(1024)S(1)} %bitcast.17, f32[3072]{0:T(1024)S(1)} %get-tuple-element.9, f32[]{:T(128)} %constant.30.clone.1), kind=kCustom, calls=%fused_computation.33 | custom fusion | bytes 24580 | tf_op jit(solution)/shard_map/scatter | solution.py:43
  81.3 1.1 copy.14
  82.4 2.7 %reshape.27 = f32[4,8,384]{2,1,0:T(8,128)} reshape(f32[6144,2]{1,0:T(8,128)S(1)} %copy.14) | data formatting | bytes 98304 | tf_op jit(solution)/shard_map/reshape | solution.py:46
  85.1 4.2 %all-to-all-start = ((f32[4,8,384]{2,1,0:T(8,128)}), f32[4,8,384]{2,1,0:T(8,128)S(1)}, u32[]{:S(2)}, u32[]{:S(2)}) async-start(f32[4,8,384]{2,1,0:T(8,128)} %reshape.27), calls=%async_computation | async-start | bytes 98304 | tf_op jit(solution)/shard_map/all_to_all | solution.py:48
  89.4 3.5 %all-to-all-done = f32[4,8,384]{2,1,0:T(8,128)S(1)} async-done(((f32[4,8,384]{2,1,0:T(8,128)}), f32[4,8,384]{2,1,0:T(8,128)S(1)}, u32[]{:S(2)}, u32[]{:S(2)}) %all-to-all-start) | async-done | bytes 49184 | tf_op jit(solution)/shard_map/all_to_all | solution.py:48
  92.8 0.6 copy.15
  93.5 3.3 %all-to-all-start.1 = ((f32[4,8,384]{2,0,1:T(4,128)}), f32[4,8,384]{2,0,1:T(4,128)S(1)}, u32[]{:S(2)}, u32[]{:S(2)}) async-start(f32[4,8,384]{2,0,1:T(4,128)} %copy.15), calls=%async_computation.1 | async-start | bytes 98304 | tf_op jit(solution)/shard_map/all_to_all | solution.py:47
  96.8 2.0 %fusion.1 = f32[1,1024]{1,0:T(1,128)S(1)} fusion(bf16[3072,1]{0,1:T(2,128)(2,1)S(1)} %reshape.72, s32[1024]{0:T(1024)S(1)} %copy-done.5, s32[3072]{0:T(1024)S(1)} %get-tuple-element.7), kind=kOutput, calls=%fused_computation.7 | convolution fusion | flops 9437184 | bytes 26624 | tf_op jit(solution)/shard_map/dot_general | solution.py:60
  98.8 8.9 %psum.14 = f32[1024]{0:T(1024)S(1)} all-reduce(f32[1024]{0:T(1024)S(1)} %bitcast.19), channel_id=1, replica_groups=mesh['row'=4,'col'=8] {'row'}, use_global_device_ids=true, to_apply=%region_5.6 | all-reduce | flops 1024 | bytes 8192 | tf_op jit(solution)/shard_map/psum | solution.py:61
  107.7 15.2 %psum.15 = f32[1024]{0:T(1024)S(1)} all-reduce(f32[1024]{0:T(1024)S(1)} %psum.14), channel_id=1, replica_groups=mesh['row'=4,'col'=8] {'col'}, use_global_device_ids=true, to_apply=%region_6.7 | all-reduce | flops 1024 | bytes 8192 | tf_op jit(solution)/shard_map/psum | solution.py:61
  123.6 3.2 %reshape.28 = f32[6144,2]{1,0:T(8,128)S(1)} reshape(f32[4,8,384]{2,1,0:T(8,128)S(1)} %copy.16) | data formatting | bytes 98304 | tf_op jit(solution)/shard_map/reshape | solution.py:54
  126.7 0.9 slice_reduce_fusion
  127.6 1.7 %fusion.5 = s32[6144]{0:T(1024)S(1)} fusion(f32[6144,2]{1,0:T(8,128)S(1)} %reshape.28), kind=kLoop, calls=%fused_computation.13 | loop fusion | flops 6144 | bytes 49152 | tf_op jit(solution)/shard_map/convert_element_type | solution.py:56
  129.3 39.4 %scatter_custom_fusion.2 = f32[2048]{0:T(1024)} fusion(s32[6144]{0:T(1024)S(1)} %fusion.5, f32[6144]{0:T(1024)S(1)} %slice_reduce_fusion, f32[]{:T(128)} %constant.30.clone.1), kind=kCustom, calls=%fused_computation.43 | custom fusion | flops 6144 | bytes 8196 | tf_op jit(solution)/shard_map/scatter-add | solution.py:55
  (21 shorter events, 1.0 us)
Async XLA Ops:
  40.1 17.5 %copy-start = (s32[3072,1]{0,1:T(1,128)S(1)}, s32[3072,1]{0,1:T(1,128)}, u32[]{:S(2)}) copy-start(s32[3072,1]{0,1:T(1,128)} %param.7) | copy-start | bytes 36868
  40.1 17.5 %copy-start.1 = (s32[3072]{0:T(1024)S(1)}, s32[3072]{0:T(1024)}, u32[]{:S(2)}) copy-start(s32[3072]{0:T(1024)} %param.9) | copy-start | bytes 36868
  40.1 17.5 %copy-start.2 = (s32[3072]{0:T(1024)S(1)}, s32[3072]{0:T(1024)}, u32[]{:S(2)}) copy-start(s32[3072]{0:T(1024)} %param.8) | copy-start | bytes 36868
  40.1 17.5 %copy-start.4 = (bf16[3072]{0:T(1024)(128)(2,1)S(1)}, bf16[3072]{0:T(1024)(128)(2,1)}, u32[]{:S(2)}) copy-start(bf16[3072]{0:T(1024)(128)(2,1)} %param.10) | copy-start | bytes 18436
  81.3 15.5 %copy-start.5 = (s32[1024]{0:T(1024)S(1)}, s32[1024]{0:T(1024)}, u32[]{:S(2)}) copy-start(s32[1024]{0:T(1024)} %param.13) | copy-start | bytes 12292
  85.1 7.7 %all-to-all-start = ((f32[4,8,384]{2,1,0:T(8,128)}), f32[4,8,384]{2,1,0:T(8,128)S(1)}, u32[]{:S(2)}, u32[]{:S(2)}) async-start(f32[4,8,384]{2,1,0:T(8,128)} %reshape.27), calls=%async_computation | async-start | bytes 98304 | tf_op jit(solution)/shard_map/all_to_all | solution.py:48
  93.5 30.1 %all-to-all-start.1 = ((f32[4,8,384]{2,0,1:T(4,128)}), f32[4,8,384]{2,0,1:T(4,128)S(1)}, u32[]{:S(2)}, u32[]{:S(2)}) async-start(f32[4,8,384]{2,0,1:T(4,128)} %copy.15), calls=%async_computation.1 | async-start | bytes 98304 | tf_op jit(solution)/shard_map/all_to_all | solution.py:47
  122.9 4.7 %copy-start.3 = (f32[1024]{0:T(1024)}, f32[1024]{0:T(1024)S(1)}, u32[]{:S(2)}) copy-start(f32[1024]{0:T(1024)S(1)} %psum.15) | copy-start | bytes 12292
